TPU v7x, 32 devices: a whole 2x2x4 slice. The times are simulated.
32 devices in a mesh: groups: 2 (over y), slab: 4 (over x, core), head: 4 (over z).
Axes of the slice: x: 2, y: 2, z: 4, core: 2. Of those that a mesh axis runs over, the one named last changes fastest.
Arguments:
- query_rows: bfloat16 [2048, 5120], P(('groups', 'slab', 'head')), parts along dimension 0, may hold values from -16 to 16
- key_rows: bfloat16 [2048, 5120], P(('groups', 'slab', 'head')), parts along dimension 0, may hold values from -16 to 16
- value_rows: bfloat16 [2048, 5120], P(('groups', 'slab', 'head')), parts along dimension 0, may hold values from -4 to 4
- tile_mask: int32 [40, 16, 5], P(None, ('groups', 'slab')), parts along dimension 1, may hold values from 0 to 1, as said below
- head_slot: int32 [40], replicated, may hold values from 0 to 39, as said below
Outputs:
- attended: bfloat16 [2048, 5120], P(('groups', 'slab', 'head')), parts along dimension 0
- slot_lse: float32 [40, 2048], P('head', ('groups', 'slab')), parts along dimension 1
There are 2 independent parts, one for each index of `groups`. A program takes and returns all parts, laid end to end along the dimension named above; an argument that names none is the same for every part. Nothing has to cross between parts.
Inputs may be any that keep to these rules, and one draw needn't show every extreme that they name: `tile_mask`: entry 2 of every row of every head is 1. `head_slot`: distinct; slots o * 10 to o * 10 + 9 belong to owner o along the head axis; every owner holds at most 10 heads and some owner holds 10.
All inputs are finite; a program needn't handle non-finite values.
Results may differ from a plain program's by a relative error of at most 0.0045.
Values may be sent and summed in bfloat16 or wider, within the bound.
A program may use at most 64 MiB of HBM per device.

v0:
```python
import functools

import jax
import jax.numpy as jnp
from jax import lax
from jax.experimental import pallas as pl
from jax.experimental.pallas import tpu as pltpu
from jax.sharding import PartitionSpec as P

MESH = pl.DeviceIdType.MESH
HEADS_PER_CHUNK = 5
FLOOR = -1e30


def attention_kernel(
    owners,
    slabs,
    dims,
    q_ref,
    k_ref,
    v_ref,
    mask_ref,
    slot_ref,
    out_ref,
    slot_lse_ref,
    q_buf,
    k_buf,
    v_buf,
    o_buf,
    lse_buf,
    mask_buf,
    slot_buf,
    in_send,
    in_recv,
    halo_send,
    halo_recv,
    out_send,
    out_recv,
    lse_send,
    lse_recv,
    small_sem,
):
    heads, head_dim, capacity, width, tok_dev, tile, reach = dims
    chunks = capacity // width
    lanes = width * head_dim
    tok_slab = tok_dev * owners
    tiles_dev = tok_slab // tile
    band = 2 * reach + 1
    halo = reach * tile
    full = heads == owners * capacity
    scale = head_dim ** (-0.5)
    me = lax.axis_index("head")
    slab = lax.axis_index("slab")
    inputs = ((k_ref, k_buf, halo), (v_ref, v_buf, halo), (q_ref, q_buf, 0))
    peers = [(sign, dist) for dist in range(owners - 1, 0, -1) for sign in (1, -1)]

    def when(condition, body):
        pl.when(condition)(body)

    def per_peer(body):
        for sign, dist in peers:
            other = me + sign * dist
            when((other >= 0) & (other < owners), functools.partial(body, other))

    def if_held(owner, chunk, body):
        if full:
            body()
        else:
            when(owner * capacity + chunk * width < heads, body)

    def columns(owner, chunk):
        first = (owner * capacity + chunk * width) * head_dim
        return pl.ds(pl.multiple_of(first, head_dim), lanes)

    def rows(owner, base):
        return pl.ds(pl.multiple_of(owner * tok_dev + base, tok_dev), tok_dev)

    def in_copy(which, chunk, src_owner, dst_owner):
        ref, buf, base = inputs[which]
        return pltpu.make_async_remote_copy(
            src_ref=ref.at[:, columns(dst_owner, chunk)],
            dst_ref=buf.at[chunk, rows(src_owner, base), :],
            send_sem=in_send.at[which, chunk, dst_owner],
            recv_sem=in_recv.at[which, chunk, src_owner],
            device_id={"head": dst_owner},
            device_id_type=MESH,
        )

    def own_copy(which, chunk):
        ref, buf, base = inputs[which]
        return pltpu.make_async_copy(
            ref.at[:, columns(me, chunk)],
            buf.at[chunk, rows(me, base), :],
            in_recv.at[which, chunk, me],
        )

    def halo_copy(which, chunk, up):
        buf = inputs[which][1]
        source = tok_slab if up else halo
        target = 0 if up else halo + tok_slab
        return pltpu.make_async_remote_copy(
            src_ref=buf.at[chunk, pl.ds(source, halo), :],
            dst_ref=buf.at[chunk, pl.ds(target, halo), :],
            send_sem=halo_send.at[which, chunk, int(up)],
            recv_sem=halo_recv.at[which, chunk, int(up)],
            device_id={"slab": slab + 1 if up else slab - 1},
            device_id_type=MESH,
        )

    def out_copy(chunk, src_owner, dst_owner):
        return pltpu.make_async_remote_copy(
            src_ref=o_buf.at[chunk, rows(dst_owner, 0), :],
            dst_ref=out_ref.at[:, columns(src_owner, chunk)],
            send_sem=out_send.at[chunk, dst_owner],
            recv_sem=out_recv.at[chunk, src_owner],
            device_id={"head": dst_owner},
            device_id_type=MESH,
        )

    def out_own(chunk):
        return pltpu.make_async_copy(
            o_buf.at[chunk, rows(me, 0), :],
            out_ref.at[:, columns(me, chunk)],
            out_recv.at[chunk, me],
        )

    def lse_copy(src_owner, dst_owner):
        return pltpu.make_async_remote_copy(
            src_ref=lse_buf.at[src_owner],
            dst_ref=lse_buf.at[src_owner],
            send_sem=lse_send.at[dst_owner],
            recv_sem=lse_recv.at[src_owner],
            device_id={"head": dst_owner},
            device_id_type=MESH,
        )

    has_up = slab < slabs - 1
    has_down = slab > 0
    barrier = pltpu.get_barrier_semaphore()

    def greet(other):
        pl.semaphore_signal(barrier, inc=1, device_id={"head": other}, device_id_type=MESH)

    per_peer(greet)

    @pl.when(has_up)
    def _():
        pl.semaphore_signal(barrier, inc=1, device_id={"slab": slab + 1}, device_id_type=MESH)

    @pl.when(has_down)
    def _():
        pl.semaphore_signal(barrier, inc=1, device_id={"slab": slab - 1}, device_id_type=MESH)

    mask_copy = pltpu.make_async_copy(mask_ref, mask_buf, small_sem.at[0])
    slot_copy = pltpu.make_async_copy(slot_ref, slot_buf, small_sem.at[1])
    mask_copy.start()
    slot_copy.start()
    pl.semaphore_wait(
        barrier, owners - 1 + has_up.astype(jnp.int32) + has_down.astype(jnp.int32)
    )

    low_half = me < owners // 2

    def send_inputs(crossing, chunk, carry):
        for which in range(3):

            def to_peer(other, which=which):
                def go():
                    if_held(other, chunk, lambda: in_copy(which, chunk, me, other).start())

                other_side = low_half != (other < owners // 2)
                when(other_side if crossing else jnp.logical_not(other_side), go)

            per_peer(to_peer)
            if crossing:
                if_held(me, chunk, lambda which=which: own_copy(which, chunk).start())
        return carry

    lax.fori_loop(0, chunks, functools.partial(send_inputs, False), 0)
    lax.fori_loop(0, chunks, functools.partial(send_inputs, True), 0)

    if not full:
        lse_buf[me] = jnp.zeros(lse_buf.shape[1:], jnp.float32)

    @pl.when(jnp.logical_not(has_down))
    def _():
        v_buf[:, :halo, :] = jnp.zeros((chunks, halo, lanes), jnp.bfloat16)

    @pl.when(jnp.logical_not(has_up))
    def _():
        v_buf[:, halo + tok_slab :, :] = jnp.zeros((chunks, halo, lanes), jnp.bfloat16)

    mask_copy.wait()
    slot_copy.wait()

    def wait_input(which, chunk):
        per_peer(lambda other: in_copy(which, chunk, other, me).wait_recv())
        own_copy(which, chunk).wait()

    def forward(chunk):
        for which in range(2):
            wait_input(which, chunk)
            when(has_up, lambda: halo_copy(which, chunk, True).start())
            when(has_down, lambda: halo_copy(which, chunk, False).start())

    def attend(chunk):
        for which in range(2):
            when(has_down, lambda: halo_copy(which, chunk, True).wait_recv())
            when(has_up, lambda: halo_copy(which, chunk, False).wait_recv())
        wait_input(2, chunk)
        for within in range(width):
            column = slice(within * head_dim, (within + 1) * head_dim)
            local_head = chunk * width + within
            global_head = me * capacity + local_head
            for block in range(tiles_dev):
                q_rows = slice(block * tile, (block + 1) * tile)
                queries = q_buf[chunk, q_rows, column]
                window = slice(block * tile, (block + band) * tile)
                keys = k_buf[chunk, window, column]
                values = v_buf[chunk, window, column]
                scores = (
                    lax.dot_general(
                        keys, queries, (((1,), (1,)), ((), ())), preferred_element_type=jnp.float32
                    )
                    * scale
                )
                parts = []
                for place in range(band):
                    key_tile = slab * tiles_dev + block + place - reach
                    inside = ((key_tile >= 0) & (key_tile < slabs * tiles_dev)).astype(jnp.int32)
                    flag = mask_buf[place, block, global_head] * inside
                    allowed = jnp.full((tile, tile), flag, jnp.int32) > 0
                    parts.append(
                        jnp.where(allowed, scores[place * tile : (place + 1) * tile], FLOOR)
                    )
                masked = jnp.concatenate(parts, axis=0)
                highest = jnp.max(masked, axis=0, keepdims=True)
                weights = jnp.exp(masked - highest)
                total = jnp.sum(weights, axis=0, keepdims=True)
                summed = lax.dot_general(
                    values,
                    weights.astype(jnp.bfloat16),
                    (((0,), (0,)), ((), ())),
                    preferred_element_type=jnp.float32,
                )
                result = jnp.transpose(summed / total)
                o_buf[chunk, q_rows, column] = result.astype(jnp.bfloat16)
                lse_buf[me, local_head, :, q_rows] = highest + jnp.log(total)

    def send_out(chunk):
        per_peer(lambda other: out_copy(chunk, me, other).start())
        out_own(chunk).start()

    if_held(me, 0, lambda: forward(0))

    def step(chunk, carry):
        if_held(me, chunk, lambda: forward(chunk))

        def finish():
            attend(chunk - 1)
            send_out(chunk - 1)

        if_held(me, chunk - 1, finish)
        return carry

    lax.fori_loop(1, chunks, step, 0)
    last = chunks - 1
    if_held(me, last, lambda: attend(last))
    per_peer(lambda other: lse_copy(me, other).start())
    if_held(me, last, lambda: send_out(last))

    per_peer(lambda other: lse_copy(other, me).wait_recv())
    slot_rows = lax.broadcasted_iota(jnp.int32, (capacity, tok_slab), 0) + me * capacity
    slot_lse = jnp.zeros((capacity, tok_slab), jnp.float32)
    for head in range(heads):
        row = jnp.broadcast_to(lse_buf[head // capacity, head % capacity], (capacity, tok_slab))
        slot_lse = jnp.where(slot_rows == slot_buf[head], row, slot_lse)
    slot_lse_ref[...] = slot_lse

    def drain(chunk, carry):
        for which in range(3):

            def sent(other, which=which):
                if_held(other, chunk, lambda: in_copy(which, chunk, me, other).wait_send())

            per_peer(sent)

        def mine():
            for which in range(2):
                when(has_up, lambda: halo_copy(which, chunk, True).wait_send())
                when(has_down, lambda: halo_copy(which, chunk, False).wait_send())
            per_peer(lambda other: out_copy(chunk, me, other).wait_send())
            out_own(chunk).wait()

        if_held(me, chunk, mine)

        def arrived(other):
            if_held(other, chunk, lambda: out_copy(chunk, other, me).wait_recv())

        per_peer(arrived)
        return carry

    lax.fori_loop(0, chunks, drain, 0)
    per_peer(lambda other: lse_copy(me, other).wait_send())


def hand_over_kernel(out_in, lse_in, out_ref, lse_ref, sems):
    copies = [
        pltpu.make_async_copy(out_in, out_ref, sems.at[0]),
        pltpu.make_async_copy(lse_in, lse_ref, sems.at[1]),
    ]
    for copy in copies:
        copy.start()
    for copy in copies:
        copy.wait()


def on_device(query_rows, key_rows, value_rows, tile_mask, head_slot):
    owners = lax.axis_size("head")
    slabs = lax.axis_size("slab")
    tok_dev, model = query_rows.shape
    heads, tiles_dev, band = tile_mask.shape
    head_dim = model // heads
    capacity = (heads + owners - 1) // owners
    reach = (band - 1) // 2
    tok_slab = tok_dev * owners
    tile = tok_slab // tiles_dev
    halo = reach * tile
    whole = heads == owners * capacity
    width = HEADS_PER_CHUNK if whole and capacity % HEADS_PER_CHUNK == 0 else 1
    chunks = capacity // width
    lanes = width * head_dim
    dims = (heads, head_dim, capacity, width, tok_dev, tile, reach)
    dma = pltpu.SemaphoreType.DMA
    anywhere = pl.BlockSpec(memory_space=pl.ANY)
    gathered, gathered_lse = pl.pallas_call(
        functools.partial(attention_kernel, owners, slabs, dims),
        out_shape=(
            jax.ShapeDtypeStruct((tok_dev, model), jnp.bfloat16),
            jax.ShapeDtypeStruct((capacity, tok_slab), jnp.float32),
        ),
        in_specs=[pl.BlockSpec(memory_space=pltpu.HBM)] * 5,
        out_specs=(pl.BlockSpec(memory_space=pltpu.VMEM), pl.BlockSpec(memory_space=pltpu.VMEM)),
        scratch_shapes=[
            pltpu.VMEM((chunks, tok_slab, lanes), jnp.bfloat16),
            pltpu.VMEM((chunks, tok_slab + 2 * halo, lanes), jnp.bfloat16),
            pltpu.VMEM((chunks, tok_slab + 2 * halo, lanes), jnp.bfloat16),
            pltpu.VMEM((chunks, tok_slab, lanes), jnp.bfloat16),
            pltpu.VMEM((owners, capacity, 1, tok_slab), jnp.float32),
            pltpu.SMEM((band, tiles_dev, heads), jnp.int32),
            pltpu.SMEM((heads,), jnp.int32),
            dma((3, chunks, owners)),
            dma((3, chunks, owners)),
            dma((2, chunks, 2)),
            dma((2, chunks, 2)),
            dma((chunks, owners)),
            dma((chunks, owners)),
            dma((owners,)),
            dma((owners,)),
            dma((2,)),
        ],
        compiler_params=pltpu.CompilerParams(collective_id=0, has_side_effects=True, vmem_limit_bytes=16 << 20),
    )(*[pltpu.with_memory_space_constraint(x, pltpu.HBM) for x in (query_rows, key_rows, value_rows, jnp.transpose(tile_mask, (2, 1, 0)), head_slot)])
    vmem = pl.BlockSpec(memory_space=pltpu.VMEM)
    hbm = pl.BlockSpec(memory_space=pltpu.HBM)
    return pl.pallas_call(
        hand_over_kernel,
        out_shape=(
            jax.ShapeDtypeStruct(gathered.shape, gathered.dtype),
            jax.ShapeDtypeStruct(gathered_lse.shape, gathered_lse.dtype),
        ),
        in_specs=[vmem, vmem],
        out_specs=(hbm, hbm),
        scratch_shapes=[dma((2,))],
        compiler_params=pltpu.CompilerParams(vmem_limit_bytes=16 << 20),
    )(gathered, gathered_lse)


def solution(mesh):
    in_specs = (
        P(("groups", "slab", "head"), None),
        P(("groups", "slab", "head"), None),
        P(("groups", "slab", "head"), None),
        P(None, ("groups", "slab"), None),
        P(),
    )
    out_specs = (P(("groups", "slab", "head"), None), P("head", ("groups", "slab")))
    return jax.shard_map(
        on_device, mesh=mesh, in_specs=in_specs, out_specs=out_specs, check_vma=False
    )
```

profile of v0, /device:TPU:9, one launch (start us, length us, event | category | flops | bytes accessed | tf_op | source)
XLA Modules:
  0.0 63.8 jit_solution(14276548057374638299)
XLA Ops:
  0.6 62.3 %shard_map.68 = (bf16[64,5120]{1,0:T(8,128)(2,1)S(1)}, f32[10,256]{1,0:T(8,128)S(1)}) custom-call(bf16[64,5120]{1,0:T(8,128)(2,1)} %q_ref.1, bf16[64,5120]{1,0:T(8,128)(2,1)} %k_ref.1, bf16[64,5120]{1,0:T(8,128)(2,1)} %v_ref.1, s32[5,2,40]{2,1,0:T(2,128)} %bitcast.1, s32[40]{0:T(128)} %slot_ref.1), custom_call_target="tpu_custom_call" | custom-call | tf_op jit(solution)/shard_map/pallas_call | solution.py:336
  62.9 0.9 %shard_map.69 = (bf16[64,5120]{1,0:T(8,128)(2,1)}, f32[10,256]{1,0:T(8,128)}) custom-call(bf16[64,5120]{1,0:T(8,128)(2,1)S(1)} %get-tuple-element.4.out_in, f32[10,256]{1,0:T(8,128)S(1)} %get-tuple-element.5.lse_in), custom_call_target="tpu_custom_call" | custom-call | tf_op jit(solution)/shard_map/pallas_call | solution.py:366
where the time goes:
time: 64.9 us; the launch traced here: 63.8 us
  Pallas kernels  63.1 us (97%)
    pallas_call x1, Pallas kernels, on_device(): pl.pallas_call(functools.partial(attention_kernel, owners, slabs, dims),...  62.3 us

commit v1 on v0

--- a/solution.py
+++ b/solution.py
@@ -8,7 +8,9 @@
 from jax.sharding import PartitionSpec as P
 
 MESH = pl.DeviceIdType.MESH
-HEADS_PER_CHUNK = 5
+HEADS_PER_CHUNK = 2
+EARLY_CHUNKS = 2
+HELD_CHUNKS = 3
 FLOOR = -1e30
 
 
@@ -304,6 +306,303 @@
     per_peer(lambda other: lse_copy(me, other).wait_send())
 
 
+def line_kernel(
+    owners,
+    slabs,
+    dims,
+    q_ref,
+    k_ref,
+    v_ref,
+    mask_ref,
+    slot_ref,
+    out_ref,
+    slot_lse_ref,
+    q_buf,
+    k_buf,
+    v_buf,
+    o_buf,
+    lse_buf,
+    lse_box,
+    mask_buf,
+    slot_buf,
+    in_send,
+    in_recv,
+    halo_send,
+    halo_recv,
+    out_send,
+    out_recv,
+    lse_send,
+    lse_recv,
+    seen,
+    small_sem,
+):
+    heads, head_dim, capacity, width, tok_dev, tile, reach = dims
+    chunks = capacity // width
+    lanes = width * head_dim
+    tok_slab = tok_dev * owners
+    tiles_dev = tok_slab // tile
+    band = 2 * reach + 1
+    halo = reach * tile
+    mid = owners // 2
+    early = min(EARLY_CHUNKS, chunks)
+    hold_from = max(chunks - HELD_CHUNKS, 0)
+    scale = head_dim ** (-0.5)
+    me = lax.axis_index("head")
+    slab = lax.axis_index("slab")
+    low = me < mid
+    inward = jnp.where(low, 1, -1)
+    inner = me + inward
+    outer = me - inward
+    across = jnp.where(low, mid, mid - 1)
+    has_up = slab < slabs - 1
+    has_down = slab > 0
+    inputs = ((k_ref, k_buf, halo), (v_ref, v_buf, halo), (q_ref, q_buf, 0))
+    peers = [(sign, dist) for dist in range(owners - 1, 0, -1) for sign in (1, -1)]
+
+    def when(condition, body):
+        pl.when(condition)(body)
+
+    def exists(other):
+        return (other >= 0) & (other < owners)
+
+    def columns(owner, chunk):
+        first = (owner * capacity + chunk * width) * head_dim
+        return pl.ds(pl.multiple_of(first, head_dim), lanes)
+
+    def rows(owner, base):
+        return pl.ds(pl.multiple_of(owner * tok_dev + base, tok_dev), tok_dev)
+
+    def wait_bytes(ref, sem):
+        pltpu.make_async_copy(ref, ref, sem).wait()
+
+    def in_copy(which, chunk, dst_owner):
+        ref, buf, base = inputs[which]
+        return pltpu.make_async_remote_copy(
+            src_ref=ref.at[:, columns(dst_owner, chunk)],
+            dst_ref=buf.at[chunk, rows(me, base), :],
+            send_sem=in_send.at[which],
+            recv_sem=in_recv.at[which, chunk],
+            device_id={"head": dst_owner},
+            device_id_type=MESH,
+        )
+
+    def own_copy(which, chunk):
+        ref, buf, base = inputs[which]
+        return pltpu.make_async_copy(
+            ref.at[:, columns(me, chunk)],
+            buf.at[chunk, rows(me, base), :],
+            in_recv.at[which, chunk],
+        )
+
+    def halo_copy(which, chunk, up):
+        buf = inputs[which][1]
+        source = tok_slab if up else halo
+        target = 0 if up else halo + tok_slab
+        return pltpu.make_async_remote_copy(
+            src_ref=buf.at[chunk, pl.ds(source, halo), :],
+            dst_ref=buf.at[chunk, pl.ds(target, halo), :],
+            send_sem=halo_send.at[which, int(up)],
+            recv_sem=halo_recv.at[which, chunk, int(up)],
+            device_id={"slab": slab + 1 if up else slab - 1},
+            device_id_type=MESH,
+        )
+
+    def out_copy(chunk, dst_owner):
+        return pltpu.make_async_remote_copy(
+            src_ref=o_buf.at[chunk, rows(dst_owner, 0), :],
+            dst_ref=out_ref.at[:, columns(me, chunk)],
+            send_sem=out_send.at[0],
+            recv_sem=out_recv.at[0],
+            device_id={"head": dst_owner},
+            device_id_type=MESH,
+        )
+
+    def out_own(chunk):
+        return pltpu.make_async_copy(
+            o_buf.at[chunk, rows(me, 0), :],
+            out_ref.at[:, columns(me, chunk)],
+            out_recv.at[0],
+        )
+
+    def lse_copy(dst_owner):
+        return pltpu.make_async_remote_copy(
+            src_ref=lse_box.at[me],
+            dst_ref=lse_box.at[me],
+            send_sem=lse_send.at[0],
+            recv_sem=lse_recv.at[0],
+            device_id={"head": dst_owner},
+            device_id_type=MESH,
+        )
+
+    barrier = pltpu.get_barrier_semaphore()
+
+    def greet(device):
+        pl.semaphore_signal(barrier, inc=1, device_id=device, device_id_type=MESH)
+
+    when(inner == across, lambda: greet({"head": inner}))
+    when(exists(outer), lambda: greet({"head": outer}))
+    when(has_up, lambda: greet({"slab": slab + 1}))
+    when(has_down, lambda: greet({"slab": slab - 1}))
+
+    mask_copy = pltpu.make_async_copy(mask_ref, mask_buf, small_sem.at[0])
+    slot_copy = pltpu.make_async_copy(slot_ref, slot_buf, small_sem.at[1])
+    mask_copy.start()
+    slot_copy.start()
+    pl.semaphore_wait(barrier, 1 + has_up.astype(jnp.int32) + has_down.astype(jnp.int32))
+
+    for chunk in range(early):
+        for which in range(3):
+            in_copy(which, chunk, inner).start()
+
+    def tell(owner, about):
+        pl.semaphore_signal(seen.at[about], inc=1, device_id={"head": owner}, device_id_type=MESH)
+
+    when(inner != across, lambda: tell(inner, me))
+    for dist in range(1, mid):
+        other = me - inward * dist
+
+        def outward(other=other, dist=dist):
+            pl.semaphore_wait(seen.at[other], 1)
+            tell(inner, other)
+            if dist == 1:
+                tell(outer, inner)
+
+        when(exists(other), outward)
+    for dist in range(2, owners):
+        other = me + inward * dist
+
+        def further(other=other):
+            pl.semaphore_wait(seen.at[other], 1)
+            when(exists(outer), lambda: tell(outer, other))
+
+        when(exists(other), further)
+
+    def send_inputs(chunk, carry):
+        for which in range(3):
+            for sign, dist in peers:
+                other = me + sign * dist
+                wanted = exists(other)
+                if dist == 1:
+                    wanted = wanted & ((other != inner) | (chunk >= early))
+                when(wanted, lambda which=which, other=other: in_copy(which, chunk, other).start())
+            own_copy(which, chunk).start()
+        return carry
+
+    lax.fori_loop(0, chunks, send_inputs, 0)
+
+    @pl.when(jnp.logical_not(has_down))
+    def _():
+        v_buf[:, :halo, :] = jnp.zeros((chunks, halo, lanes), jnp.bfloat16)
+
+    @pl.when(jnp.logical_not(has_up))
+    def _():
+        v_buf[:, halo + tok_slab :, :] = jnp.zeros((chunks, halo, lanes), jnp.bfloat16)
+
+    mask_copy.wait()
+    slot_copy.wait()
+
+    def wait_input(which, chunk):
+        _, buf, base = inputs[which]
+        wait_bytes(buf.at[chunk, pl.ds(base, tok_slab), :], in_recv.at[which, chunk])
+
+    def forward(chunk):
+        for which in range(2):
+            wait_input(which, chunk)
+            when(has_up, lambda which=which: halo_copy(which, chunk, True).start())
+            when(has_down, lambda which=which: halo_copy(which, chunk, False).start())
+
+    def attend(chunk):
+        for which in range(2):
+            when(has_down, lambda which=which: halo_copy(which, chunk, True).wait_recv())
+            when(has_up, lambda which=which: halo_copy(which, chunk, False).wait_recv())
+        wait_input(2, chunk)
+        for within in range(width):
+            column = slice(within * head_dim, (within + 1) * head_dim)
+            local_head = chunk * width + within
+            global_head = me * capacity + local_head
+            for block in range(tiles_dev):
+                q_rows = slice(block * tile, (block + 1) * tile)
+                queries = q_buf[chunk, q_rows, column]
+                window = slice(block * tile, (block + band) * tile)
+                keys = k_buf[chunk, window, column]
+                values = v_buf[chunk, window, column]
+                scores = (
+                    lax.dot_general(
+                        keys, queries, (((1,), (1,)), ((), ())), preferred_element_type=jnp.float32
+                    )
+                    * scale
+                )
+                parts = []
+                for place in range(band):
+                    key_tile = slab * tiles_dev + block + place - reach
+                    inside = ((key_tile >= 0) & (key_tile < slabs * tiles_dev)).astype(jnp.int32)
+                    flag = mask_buf[place, block, global_head] * inside
+                    allowed = jnp.full((tile, tile), flag, jnp.int32) > 0
+                    parts.append(
+                        jnp.where(allowed, scores[place * tile : (place + 1) * tile], FLOOR)
+                    )
+                masked = jnp.concatenate(parts, axis=0)
+                highest = jnp.max(masked, axis=0, keepdims=True)
+                weights = jnp.exp(masked - highest)
+                total = jnp.sum(weights, axis=0, keepdims=True)
+                summed = lax.dot_general(
+                    values,
+                    weights.astype(jnp.bfloat16),
+                    (((0,), (0,)), ((), ())),
+                    preferred_element_type=jnp.float32,
+                )
+                result = jnp.transpose(summed / total)
+                o_buf[chunk, q_rows, column] = result.astype(jnp.bfloat16)
+                lse_buf[local_head, :, q_rows] = highest + jnp.log(total)
+
+    def send_out(chunk):
+        for sign, dist in peers:
+            other = me + sign * dist
+            wanted = exists(other) & ((other != across) | (chunk < hold_from))
+            when(wanted, lambda other=other: out_copy(chunk, other).start())
+        out_own(chunk).start()
+
+    forward(0)
+
+    def step(chunk, carry):
+        when(chunk < chunks, lambda: forward(chunk))
+        attend(chunk - 1)
+        send_out(chunk - 1)
+        return carry
+
+    lax.fori_loop(1, chunks + 1, step, 0)
+
+    own_lse = lse_buf[...].reshape(capacity, tok_slab)
+    lse_box[me] = own_lse.astype(jnp.bfloat16)
+    for sign, dist in peers:
+        other = me + sign * dist
+        when(exists(other), lambda other=other: lse_copy(other).start())
+    for chunk in range(hold_from, chunks):
+        out_copy(chunk, across).start()
+
+    wait_bytes(lse_box.at[pl.ds(0, owners - 1)], lse_recv.at[0])
+    slot_rows = lax.broadcasted_iota(jnp.int32, (capacity, tok_slab), 0) + me * capacity
+    slot_lse = jnp.zeros((capacity, tok_slab), jnp.float32)
+    for owner in range(owners):
+        own = jnp.full((capacity, tok_slab), (me == owner).astype(jnp.int32)) > 0
+        theirs = jnp.where(own, own_lse, lse_box[owner].astype(jnp.float32))
+        for within in range(capacity):
+            row = jnp.broadcast_to(theirs[within : within + 1], (capacity, tok_slab))
+            slot_lse = jnp.where(slot_rows == slot_buf[owner * capacity + within], row, slot_lse)
+    slot_lse_ref[...] = slot_lse
+
+    others = (owners - 1) * capacity * head_dim
+    for which in range(3):
+        wait_bytes(inputs[which][0].at[:, pl.ds(0, others)], in_send.at[which])
+    for which in range(2):
+        edge = inputs[which][1].at[:, pl.ds(0, halo), :]
+        when(has_up, lambda which=which, edge=edge: wait_bytes(edge, halo_send.at[which, 1]))
+        when(has_down, lambda which=which, edge=edge: wait_bytes(edge, halo_send.at[which, 0]))
+    wait_bytes(lse_box.at[pl.ds(0, owners - 1)], lse_send.at[0])
+    wait_bytes(o_buf.at[:, pl.ds(0, (owners - 1) * tok_dev), :], out_send.at[0])
+    wait_bytes(out_ref, out_recv.at[0])
+
+
 def hand_over_kernel(out_in, lse_in, out_ref, lse_ref, sems):
     copies = [
         pltpu.make_async_copy(out_in, out_ref, sems.at[0]),
@@ -327,28 +626,46 @@
     tile = tok_slab // tiles_dev
     halo = reach * tile
     whole = heads == owners * capacity
+    line = whole and owners % 2 == 0
     width = HEADS_PER_CHUNK if whole and capacity % HEADS_PER_CHUNK == 0 else 1
     chunks = capacity // width
     lanes = width * head_dim
     dims = (heads, head_dim, capacity, width, tok_dev, tile, reach)
     dma = pltpu.SemaphoreType.DMA
-    anywhere = pl.BlockSpec(memory_space=pl.ANY)
-    gathered, gathered_lse = pl.pallas_call(
-        functools.partial(attention_kernel, owners, slabs, dims),
-        out_shape=(
-            jax.ShapeDtypeStruct((tok_dev, model), jnp.bfloat16),
-            jax.ShapeDtypeStruct((capacity, tok_slab), jnp.float32),
-        ),
-        in_specs=[pl.BlockSpec(memory_space=pltpu.HBM)] * 5,
-        out_specs=(pl.BlockSpec(memory_space=pltpu.VMEM), pl.BlockSpec(memory_space=pltpu.VMEM)),
-        scratch_shapes=[
-            pltpu.VMEM((chunks, tok_slab, lanes), jnp.bfloat16),
-            pltpu.VMEM((chunks, tok_slab + 2 * halo, lanes), jnp.bfloat16),
-            pltpu.VMEM((chunks, tok_slab + 2 * halo, lanes), jnp.bfloat16),
-            pltpu.VMEM((chunks, tok_slab, lanes), jnp.bfloat16),
+    buffers = [
+        pltpu.VMEM((chunks, tok_slab, lanes), jnp.bfloat16),
+        pltpu.VMEM((chunks, tok_slab + 2 * halo, lanes), jnp.bfloat16),
+        pltpu.VMEM((chunks, tok_slab + 2 * halo, lanes), jnp.bfloat16),
+        pltpu.VMEM((chunks, tok_slab, lanes), jnp.bfloat16),
+    ]
+    tables = [
+        pltpu.SMEM((band, tiles_dev, heads), jnp.int32),
+        pltpu.SMEM((heads,), jnp.int32),
+    ]
+    if line:
+        kernel = line_kernel
+        scratch = [
+            *buffers,
+            pltpu.VMEM((capacity, 1, tok_slab), jnp.float32),
+            pltpu.VMEM((owners, capacity, tok_slab), jnp.bfloat16),
+            *tables,
+            dma((3,)),
+            dma((3, chunks)),
+            dma((2, 2)),
+            dma((2, chunks, 2)),
+            dma((1,)),
+            dma((1,)),
+            dma((1,)),
+            dma((1,)),
+            pltpu.SemaphoreType.REGULAR((owners,)),
+            dma((2,)),
+        ]
+    else:
+        kernel = attention_kernel
+        scratch = [
+            *buffers,
             pltpu.VMEM((owners, capacity, 1, tok_slab), jnp.float32),
-            pltpu.SMEM((band, tiles_dev, heads), jnp.int32),
-            pltpu.SMEM((heads,), jnp.int32),
+            *tables,
             dma((3, chunks, owners)),
             dma((3, chunks, owners)),
             dma((2, chunks, 2)),
@@ -358,7 +675,16 @@
             dma((owners,)),
             dma((owners,)),
             dma((2,)),
-        ],
+        ]
+    gathered, gathered_lse = pl.pallas_call(
+        functools.partial(kernel, owners, slabs, dims),
+        out_shape=(
+            jax.ShapeDtypeStruct((tok_dev, model), jnp.bfloat16),
+            jax.ShapeDtypeStruct((capacity, tok_slab), jnp.float32),
+        ),
+        in_specs=[pl.BlockSpec(memory_space=pltpu.HBM)] * 5,
+        out_specs=(pl.BlockSpec(memory_space=pltpu.VMEM), pl.BlockSpec(memory_space=pltpu.VMEM)),
+        scratch_shapes=scratch,
         compiler_params=pltpu.CompilerParams(collective_id=0, has_side_effects=True, vmem_limit_bytes=16 << 20),
     )(*[pltpu.with_memory_space_constraint(x, pltpu.HBM) for x in (query_rows, key_rows, value_rows, jnp.transpose(tile_mask, (2, 1, 0)), head_slot)])
     vmem = pl.BlockSpec(memory_space=pltpu.VMEM)

time: 64.9 us -> 62.9 us (0.969); the launches traced: 63.8 us -> 62.6 us
  Pallas kernels: 63.1 us -> 62 us
    pallas_call x1, Pallas kernels: 62.3 us -> 61.1 us  [on_device(): pl.pallas_call(functools.partial(kernel, owners, slabs, dims), out_shape=...]
where the time goes in v1:
time: 62.9 us; the launch traced here: 62.6 us
  Pallas kernels  62 us (99%)
  between operations  0.64 us (1%)
    pallas_call x1, Pallas kernels, on_device(): pl.pallas_call(functools.partial(kernel, owners, slabs, dims), out_shape=...  61.1 us

profile of v1, /device:TPU:9, one launch (start us, length us, event | category | flops | bytes accessed | tf_op | source)
XLA Modules:
  0.0 62.6 jit_solution(15246203005367176527)
XLA Ops:
  0.6 61.1 %shard_map.68 = (bf16[64,5120]{1,0:T(8,128)(2,1)S(1)}, f32[10,256]{1,0:T(8,128)S(1)}) custom-call(bf16[64,5120]{1,0:T(8,128)(2,1)} %q_ref.1, bf16[64,5120]{1,0:T(8,128)(2,1)} %k_ref.1, bf16[64,5120]{1,0:T(8,128)(2,1)} %v_ref.1, s32[5,2,40]{2,1,0:T(2,128)} %bitcast.1, s32[40]{0:T(128)} %slot_ref.1), custom_call_target="tpu_custom_call" | custom-call | tf_op jit(solution)/shard_map/pallas_call | solution.py:679
  61.8 0.9 %shard_map.69 = (bf16[64,5120]{1,0:T(8,128)(2,1)}, f32[10,256]{1,0:T(8,128)}) custom-call(bf16[64,5120]{1,0:T(8,128)(2,1)S(1)} %get-tuple-element.4.out_in, f32[10,256]{1,0:T(8,128)S(1)} %get-tuple-element.5.lse_in), custom_call_target="tpu_custom_call" | custom-call | tf_op jit(solution)/shard_map/pallas_call | solution.py:692

commit v2 on v1

--- a/solution.py
+++ b/solution.py
@@ -10,7 +10,7 @@
 MESH = pl.DeviceIdType.MESH
 HEADS_PER_CHUNK = 2
 EARLY_CHUNKS = 2
-HELD_CHUNKS = 3
+HELD_CHUNKS = 4
 FLOOR = -1e30
 
 
@@ -323,6 +323,7 @@
     o_buf,
     lse_buf,
     lse_box,
+    last_box,
     mask_buf,
     slot_buf,
     in_send,
@@ -346,6 +347,7 @@
     mid = owners // 2
     early = min(EARLY_CHUNKS, chunks)
     hold_from = max(chunks - HELD_CHUNKS, 0)
+    first_rows = (capacity - width) * tiles_dev
     scale = head_dim ** (-0.5)
     me = lax.axis_index("head")
     slab = lax.axis_index("slab")
@@ -424,12 +426,33 @@
             out_recv.at[0],
         )
 
-    def lse_copy(dst_owner):
+    def lse_copy(dst_owner, crossing):
         return pltpu.make_async_remote_copy(
             src_ref=lse_box.at[me],
             dst_ref=lse_box.at[me],
-            send_sem=lse_send.at[0],
-            recv_sem=lse_recv.at[0],
+            send_sem=lse_send.at[owners],
+            recv_sem=lse_recv.at[int(crossing)],
+            device_id={"head": dst_owner},
+            device_id_type=MESH,
+        )
+
+    def lse_relay(dst_owner):
+        boxes = lse_box.at[pl.ds(jnp.where(low, mid, 0), mid)]
+        return pltpu.make_async_remote_copy(
+            src_ref=boxes,
+            dst_ref=boxes,
+            send_sem=lse_send.at[dst_owner],
+            recv_sem=lse_recv.at[1],
+            device_id={"head": dst_owner},
+            device_id_type=MESH,
+        )
+
+    def last_copy(dst_owner):
+        return pltpu.make_async_remote_copy(
+            src_ref=last_box.at[me],
+            dst_ref=last_box.at[me],
+            send_sem=lse_send.at[owners + 1],
+            recv_sem=lse_recv.at[2],
             device_id={"head": dst_owner},
             device_id_type=MESH,
         )
@@ -498,6 +521,7 @@
     def _():
         v_buf[:, halo + tok_slab :, :] = jnp.zeros((chunks, halo, lanes), jnp.bfloat16)
 
+    lse_buf[...] = jnp.zeros(lse_buf.shape, jnp.float32)
     mask_copy.wait()
     slot_copy.wait()
 
@@ -553,7 +577,8 @@
                 )
                 result = jnp.transpose(summed / total)
                 o_buf[chunk, q_rows, column] = result.astype(jnp.bfloat16)
-                lse_buf[local_head, :, q_rows] = highest + jnp.log(total)
+                row = local_head * tiles_dev + block
+                lse_buf[pl.ds(row, 1), :] = highest + jnp.log(total)
 
     def send_out(chunk):
         for sign, dist in peers:
@@ -562,34 +587,62 @@
             when(wanted, lambda other=other: out_copy(chunk, other).start())
         out_own(chunk).start()
 
+    side = jnp.where(low, 0, mid)
+    mates = [(sign, dist) for dist in range(mid - 1, 0, -1) for sign in (1, -1)]
+
+    def per_mate(body):
+        for sign, dist in mates:
+            other = me + sign * dist
+            when((other >= side) & (other < side + mid), functools.partial(body, other))
+
+    def send_lse():
+        lse_box[me] = lse_buf[:first_rows, :].astype(jnp.bfloat16)
+        lse_copy(across, True).start()
+        per_mate(lambda other: lse_copy(other, False).start())
+
     forward(0)
 
     def step(chunk, carry):
         when(chunk < chunks, lambda: forward(chunk))
         attend(chunk - 1)
+        when(chunk == chunks - 1, send_lse)
         send_out(chunk - 1)
         return carry
 
     lax.fori_loop(1, chunks + 1, step, 0)
 
-    own_lse = lse_buf[...].reshape(capacity, tok_slab)
-    lse_box[me] = own_lse.astype(jnp.bfloat16)
+    last_box[me] = lse_buf[first_rows:, :].astype(jnp.bfloat16)
     for sign, dist in peers:
         other = me + sign * dist
-        when(exists(other), lambda other=other: lse_copy(other).start())
+        when(exists(other), lambda other=other: last_copy(other).start())
     for chunk in range(hold_from, chunks):
         out_copy(chunk, across).start()
 
-    wait_bytes(lse_box.at[pl.ds(0, owners - 1)], lse_recv.at[0])
-    slot_rows = lax.broadcasted_iota(jnp.int32, (capacity, tok_slab), 0) + me * capacity
-    slot_lse = jnp.zeros((capacity, tok_slab), jnp.float32)
+    half = lse_box.at[pl.ds(0, mid)]
+    wait_bytes(half, lse_recv.at[1])
+    when(inner == across, lambda: per_mate(lambda other: lse_relay(other).start()))
+    if mid > 1:
+        wait_bytes(lse_box.at[pl.ds(0, mid - 1)], lse_recv.at[0])
+    wait_bytes(last_box.at[pl.ds(0, owners - 1)], lse_recv.at[2])
+    slot_rows = lax.broadcasted_iota(jnp.int32, (capacity, tile), 0) + me * capacity
+    slot_lse = [jnp.zeros((capacity, tile), jnp.float32) for _ in range(tiles_dev)]
     for owner in range(owners):
-        own = jnp.full((capacity, tok_slab), (me == owner).astype(jnp.int32)) > 0
-        theirs = jnp.where(own, own_lse, lse_box[owner].astype(jnp.float32))
-        for within in range(capacity):
-            row = jnp.broadcast_to(theirs[within : within + 1], (capacity, tok_slab))
-            slot_lse = jnp.where(slot_rows == slot_buf[owner * capacity + within], row, slot_lse)
-    slot_lse_ref[...] = slot_lse
+        mine = (me == owner).astype(jnp.int32)
+
+        def values(own, box, owner=owner, mine=mine):
+            return jnp.where(jnp.full(own.shape, mine) > 0, own, box[owner].astype(jnp.float32))
+
+        theirs = values(lse_buf[:first_rows, :], lse_box)
+        last = values(lse_buf[first_rows:, :], last_box)
+        for head in range(capacity):
+            here = slot_rows == slot_buf[owner * capacity + head]
+            source, first = (theirs, 0) if head < capacity - width else (last, capacity - width)
+            for block in range(tiles_dev):
+                row = (head - first) * tiles_dev + block
+                row = jnp.broadcast_to(source[row : row + 1], (capacity, tile))
+                slot_lse[block] = jnp.where(here, row, slot_lse[block])
+    for block in range(tiles_dev):
+        slot_lse_ref[:, block * tile : (block + 1) * tile] = slot_lse[block]
 
     others = (owners - 1) * capacity * head_dim
     for which in range(3):
@@ -598,7 +651,9 @@
         edge = inputs[which][1].at[:, pl.ds(0, halo), :]
         when(has_up, lambda which=which, edge=edge: wait_bytes(edge, halo_send.at[which, 1]))
         when(has_down, lambda which=which, edge=edge: wait_bytes(edge, halo_send.at[which, 0]))
-    wait_bytes(lse_box.at[pl.ds(0, owners - 1)], lse_send.at[0])
+    wait_bytes(half, lse_send.at[owners])
+    when(inner == across, lambda: per_mate(lambda other: lse_relay(other).wait_send()))
+    wait_bytes(last_box.at[pl.ds(0, owners - 1)], lse_send.at[owners + 1])
     wait_bytes(o_buf.at[:, pl.ds(0, (owners - 1) * tok_dev), :], out_send.at[0])
     wait_bytes(out_ref, out_recv.at[0])
 
@@ -626,9 +681,9 @@
     tile = tok_slab // tiles_dev
     halo = reach * tile
     whole = heads == owners * capacity
-    line = whole and owners % 2 == 0
     width = HEADS_PER_CHUNK if whole and capacity % HEADS_PER_CHUNK == 0 else 1
     chunks = capacity // width
+    line = whole and owners % 2 == 0 and chunks > 1
     lanes = width * head_dim
     dims = (heads, head_dim, capacity, width, tok_dev, tile, reach)
     dma = pltpu.SemaphoreType.DMA
@@ -644,10 +699,13 @@
     ]
     if line:
         kernel = line_kernel
+        first_rows = (capacity - width) * tiles_dev
+        last_rows = -(-width * tiles_dev // 8) * 8
         scratch = [
             *buffers,
-            pltpu.VMEM((capacity, 1, tok_slab), jnp.float32),
-            pltpu.VMEM((owners, capacity, tok_slab), jnp.bfloat16),
+            pltpu.VMEM((first_rows + last_rows, tile), jnp.float32),
+            pltpu.VMEM((owners, first_rows, tile), jnp.bfloat16),
+            pltpu.VMEM((owners, last_rows, tile), jnp.bfloat16),
             *tables,
             dma((3,)),
             dma((3, chunks)),
@@ -655,8 +713,8 @@
             dma((2, chunks, 2)),
             dma((1,)),
             dma((1,)),
-            dma((1,)),
-            dma((1,)),
+            dma((owners + 2,)),
+            dma((3,)),
             pltpu.SemaphoreType.REGULAR((owners,)),
             dma((2,)),
         ]

time: 62.9 us -> 62.5 us (level)
  no operation moved by 1% of the time
where the time goes in v2:
time: 62.5 us; the launch traced here: 62.4 us
  Pallas kernels  61.7 us (99%)
  between operations  0.64 us (1%)
    pallas_call x1, Pallas kernels, on_device(): pl.pallas_call(functools.partial(kernel, owners, slabs, dims), out_shape=...  60.9 us

profile of v2, /device:TPU:9, one launch (start us, length us, event | category | flops | bytes accessed | tf_op | source)
XLA Modules:
  0.0 62.4 jit_solution(3018693404589041241)
XLA Ops:
  0.6 60.9 %shard_map.68 = (bf16[64,5120]{1,0:T(8,128)(2,1)S(1)}, f32[10,256]{1,0:T(8,128)S(1)}) custom-call(bf16[64,5120]{1,0:T(8,128)(2,1)} %q_ref.1, bf16[64,5120]{1,0:T(8,128)(2,1)} %k_ref.1, bf16[64,5120]{1,0:T(8,128)(2,1)} %v_ref.1, s32[5,2,40]{2,1,0:T(2,128)} %bitcast.1, s32[40]{0:T(128)} %slot_ref.1), custom_call_target="tpu_custom_call" | custom-call | tf_op jit(solution)/shard_map/pallas_call | solution.py:737
  61.5 0.9 %shard_map.69 = (bf16[64,5120]{1,0:T(8,128)(2,1)}, f32[10,256]{1,0:T(8,128)}) custom-call(bf16[64,5120]{1,0:T(8,128)(2,1)S(1)} %get-tuple-element.4.out_in, f32[10,256]{1,0:T(8,128)S(1)} %get-tuple-element.5.lse_in), custom_call_target="tpu_custom_call" | custom-call | tf_op jit(solution)/shard_map/pallas_call | solution.py:750

commit v3 on v2

--- a/solution.py
+++ b/solution.py
@@ -335,6 +335,7 @@
     lse_send,
     lse_recv,
     seen,
+    beside,
     small_sem,
 ):
     heads, head_dim, capacity, width, tok_dev, tile, reach = dims
@@ -464,14 +465,17 @@
 
     when(inner == across, lambda: greet({"head": inner}))
     when(exists(outer), lambda: greet({"head": outer}))
-    when(has_up, lambda: greet({"slab": slab + 1}))
-    when(has_down, lambda: greet({"slab": slab - 1}))
+    at_end = jnp.logical_not(exists(outer))
+    end_up = at_end & has_up
+    end_down = at_end & has_down
+    when(end_up, lambda: greet({"slab": slab + 1}))
+    when(end_down, lambda: greet({"slab": slab - 1}))
 
     mask_copy = pltpu.make_async_copy(mask_ref, mask_buf, small_sem.at[0])
     slot_copy = pltpu.make_async_copy(slot_ref, slot_buf, small_sem.at[1])
     mask_copy.start()
     slot_copy.start()
-    pl.semaphore_wait(barrier, 1 + has_up.astype(jnp.int32) + has_down.astype(jnp.int32))
+    pl.semaphore_wait(barrier, 1 + end_up.astype(jnp.int32) + end_down.astype(jnp.int32))
 
     for chunk in range(early):
         for which in range(3):
@@ -499,6 +503,12 @@
             when(exists(outer), lambda: tell(outer, other))
 
         when(exists(other), further)
+
+    def tell_beside(which, device):
+        pl.semaphore_signal(beside.at[which], inc=1, device_id=device, device_id_type=MESH)
+
+    when(end_up, lambda: tell_beside(0, {"slab": slab + 1}))
+    when(end_down, lambda: tell_beside(1, {"slab": slab - 1}))
 
     def send_inputs(chunk, carry):
         for which in range(3):
@@ -522,6 +532,14 @@
         v_buf[:, halo + tok_slab :, :] = jnp.zeros((chunks, halo, lanes), jnp.bfloat16)
 
     lse_buf[...] = jnp.zeros(lse_buf.shape, jnp.float32)
+    for which, there in ((0, has_down), (1, has_up)):
+
+        def hear(which=which):
+            pl.semaphore_wait(beside.at[which], 1)
+            when(inner != across, lambda: tell_beside(which, {"head": inner}))
+
+        when(there, hear)
+
     mask_copy.wait()
     slot_copy.wait()
 
@@ -716,6 +734,7 @@
             dma((owners + 2,)),
             dma((3,)),
             pltpu.SemaphoreType.REGULAR((owners,)),
+            pltpu.SemaphoreType.REGULAR((2,)),
             dma((2,)),
         ]
     else:

time: 62.5 us -> 62.5 us (level)
  no operation moved by 1% of the time
where the time goes in v3:
time: 62.5 us; the launch traced here: 62.1 us
  Pallas kernels  61.4 us (98%)
  between operations  0.64 us (1%)
    pallas_call x1, Pallas kernels, on_device(): pl.pallas_call(functools.partial(kernel, owners, slabs, dims), out_shape=...  60.6 us

profile of v3, /device:TPU:9, one launch (start us, length us, event | category | flops | bytes accessed | tf_op | source)
XLA Modules:
  0.0 62.1 jit_solution(13488459229447879993)
XLA Ops:
  0.6 60.6 %shard_map.68 = (bf16[64,5120]{1,0:T(8,128)(2,1)S(1)}, f32[10,256]{1,0:T(8,128)S(1)}) custom-call(bf16[64,5120]{1,0:T(8,128)(2,1)} %q_ref.1, bf16[64,5120]{1,0:T(8,128)(2,1)} %k_ref.1, bf16[64,5120]{1,0:T(8,128)(2,1)} %v_ref.1, s32[5,2,40]{2,1,0:T(2,128)} %bitcast.1, s32[40]{0:T(128)} %slot_ref.1), custom_call_target="tpu_custom_call" | custom-call | tf_op jit(solution)/shard_map/pallas_call | solution.py:756
  61.2 0.9 %shard_map.69 = (bf16[64,5120]{1,0:T(8,128)(2,1)}, f32[10,256]{1,0:T(8,128)}) custom-call(bf16[64,5120]{1,0:T(8,128)(2,1)S(1)} %get-tuple-element.4.out_in, f32[10,256]{1,0:T(8,128)S(1)} %get-tuple-element.5.lse_in), custom_call_target="tpu_custom_call" | custom-call | tf_op jit(solution)/shard_map/pallas_call | solution.py:769

commit v4 on v3

--- a/solution.py
+++ b/solution.py
@@ -10,7 +10,8 @@
 MESH = pl.DeviceIdType.MESH
 HEADS_PER_CHUNK = 2
 EARLY_CHUNKS = 2
-HELD_CHUNKS = 4
+QUERY_LAG = 0
+HELD_CHUNKS = 3
 FLOOR = -1e30
 
 
@@ -510,18 +511,27 @@
     when(end_up, lambda: tell_beside(0, {"slab": slab + 1}))
     when(end_down, lambda: tell_beside(1, {"slab": slab - 1}))
 
+    def send_input(which, chunk):
+        for sign, dist in peers:
+            other = me + sign * dist
+            wanted = exists(other)
+            if dist == 1:
+                wanted = wanted & ((other != inner) | (chunk >= early))
+            when(wanted, lambda other=other: in_copy(which, chunk, other).start())
+        own_copy(which, chunk).start()
+
+    lead = min(QUERY_LAG, chunks)
+
     def send_inputs(chunk, carry):
-        for which in range(3):
-            for sign, dist in peers:
-                other = me + sign * dist
-                wanted = exists(other)
-                if dist == 1:
-                    wanted = wanted & ((other != inner) | (chunk >= early))
-                when(wanted, lambda which=which, other=other: in_copy(which, chunk, other).start())
-            own_copy(which, chunk).start()
+        def ahead():
+            send_input(0, chunk)
+            send_input(1, chunk)
+
+        when(chunk < chunks, ahead)
+        when(chunk >= lead, lambda: send_input(2, chunk - lead))
         return carry
 
-    lax.fori_loop(0, chunks, send_inputs, 0)
+    lax.fori_loop(0, chunks + lead, send_inputs, 0)
 
     @pl.when(jnp.logical_not(has_down))
     def _():

time: 62.5 us -> 61.6 us (0.986)
  no operation moved by 1% of the time
where the time goes in v4:
time: 61.6 us; the launch traced here: 61.5 us
  Pallas kernels  60.8 us (99%)
  between operations  0.64 us (1%)
    pallas_call x1, Pallas kernels, on_device(): pl.pallas_call(functools.partial(kernel, owners, slabs, dims), out_shape=...  60 us

profile of v4, /device:TPU:9, one launch (start us, length us, event | category | flops | bytes accessed | tf_op | source)
XLA Modules:
  0.0 61.5 jit_solution(17604631541005269740)
XLA Ops:
  0.6 60.0 %shard_map.68 = (bf16[64,5120]{1,0:T(8,128)(2,1)S(1)}, f32[10,256]{1,0:T(8,128)S(1)}) custom-call(bf16[64,5120]{1,0:T(8,128)(2,1)} %q_ref.1, bf16[64,5120]{1,0:T(8,128)(2,1)} %k_ref.1, bf16[64,5120]{1,0:T(8,128)(2,1)} %v_ref.1, s32[5,2,40]{2,1,0:T(2,128)} %bitcast.1, s32[40]{0:T(128)} %slot_ref.1), custom_call_target="tpu_custom_call" | custom-call | tf_op jit(solution)/shard_map/pallas_call | solution.py:766
  60.6 0.9 %shard_map.69 = (bf16[64,5120]{1,0:T(8,128)(2,1)}, f32[10,256]{1,0:T(8,128)}) custom-call(bf16[64,5120]{1,0:T(8,128)(2,1)S(1)} %get-tuple-element.4.out_in, f32[10,256]{1,0:T(8,128)S(1)} %get-tuple-element.5.lse_in), custom_call_target="tpu_custom_call" | custom-call | tf_op jit(solution)/shard_map/pallas_call | solution.py:779

commit v5 on v4

--- a/solution.py
+++ b/solution.py
@@ -9,7 +9,7 @@
 
 MESH = pl.DeviceIdType.MESH
 HEADS_PER_CHUNK = 2
-EARLY_CHUNKS = 2
+EARLY_CHUNKS = 3
 QUERY_LAG = 0
 HELD_CHUNKS = 3
 FLOOR = -1e30
@@ -319,8 +319,7 @@
     out_ref,
     slot_lse_ref,
     q_buf,
-    k_buf,
-    v_buf,
+    kv_buf,
     o_buf,
     lse_buf,
     lse_box,
@@ -360,7 +359,7 @@
     across = jnp.where(low, mid, mid - 1)
     has_up = slab < slabs - 1
     has_down = slab > 0
-    inputs = ((k_ref, k_buf, halo), (v_ref, v_buf, halo), (q_ref, q_buf, 0))
+    inputs = ((k_ref, kv_buf.at[0], halo), (v_ref, kv_buf.at[1], halo), (q_ref, q_buf, 0))
     peers = [(sign, dist) for dist in range(owners - 1, 0, -1) for sign in (1, -1)]
 
     def when(condition, body):
@@ -384,7 +383,7 @@
         return pltpu.make_async_remote_copy(
             src_ref=ref.at[:, columns(dst_owner, chunk)],
             dst_ref=buf.at[chunk, rows(me, base), :],
-            send_sem=in_send.at[which],
+            send_sem=in_send.at[0],
             recv_sem=in_recv.at[which, chunk],
             device_id={"head": dst_owner},
             device_id_type=MESH,
@@ -399,17 +398,21 @@
         )
 
     def halo_copy(which, chunk, up):
-        buf = inputs[which][1]
         source = tok_slab if up else halo
         target = 0 if up else halo + tok_slab
         return pltpu.make_async_remote_copy(
-            src_ref=buf.at[chunk, pl.ds(source, halo), :],
-            dst_ref=buf.at[chunk, pl.ds(target, halo), :],
-            send_sem=halo_send.at[which, int(up)],
-            recv_sem=halo_recv.at[which, chunk, int(up)],
+            src_ref=kv_buf.at[which, chunk, pl.ds(source, halo), :],
+            dst_ref=kv_buf.at[which, chunk, pl.ds(target, halo), :],
+            send_sem=halo_send.at[0],
+            recv_sem=halo_recv.at[chunk],
             device_id={"slab": slab + 1 if up else slab - 1},
             device_id_type=MESH,
         )
+
+    def per_sides(body):
+        both = has_up & has_down
+        when(both, lambda: body(2))
+        when(jnp.logical_not(both) & (has_up | has_down), lambda: body(1))
 
     def out_copy(chunk, dst_owner):
         return pltpu.make_async_remote_copy(
@@ -432,7 +435,7 @@
         return pltpu.make_async_remote_copy(
             src_ref=lse_box.at[me],
             dst_ref=lse_box.at[me],
-            send_sem=lse_send.at[owners],
+            send_sem=lse_send.at[0],
             recv_sem=lse_recv.at[int(crossing)],
             device_id={"head": dst_owner},
             device_id_type=MESH,
@@ -443,7 +446,7 @@
         return pltpu.make_async_remote_copy(
             src_ref=boxes,
             dst_ref=boxes,
-            send_sem=lse_send.at[dst_owner],
+            send_sem=lse_send.at[1],
             recv_sem=lse_recv.at[1],
             device_id={"head": dst_owner},
             device_id_type=MESH,
@@ -453,7 +456,7 @@
         return pltpu.make_async_remote_copy(
             src_ref=last_box.at[me],
             dst_ref=last_box.at[me],
-            send_sem=lse_send.at[owners + 1],
+            send_sem=lse_send.at[2],
             recv_sem=lse_recv.at[2],
             device_id={"head": dst_owner},
             device_id_type=MESH,
@@ -505,11 +508,11 @@
 
         when(exists(other), further)
 
-    def tell_beside(which, device):
-        pl.semaphore_signal(beside.at[which], inc=1, device_id=device, device_id_type=MESH)
-
-    when(end_up, lambda: tell_beside(0, {"slab": slab + 1}))
-    when(end_down, lambda: tell_beside(1, {"slab": slab - 1}))
+    def tell_beside(device):
+        pl.semaphore_signal(beside.at[0], inc=1, device_id=device, device_id_type=MESH)
+
+    when(end_up, lambda: tell_beside({"slab": slab + 1}))
+    when(end_down, lambda: tell_beside({"slab": slab - 1}))
 
     def send_input(which, chunk):
         for sign, dist in peers:
@@ -535,39 +538,30 @@
 
     @pl.when(jnp.logical_not(has_down))
     def _():
-        v_buf[:, :halo, :] = jnp.zeros((chunks, halo, lanes), jnp.bfloat16)
+        kv_buf[1, :, :halo, :] = jnp.zeros((chunks, halo, lanes), jnp.bfloat16)
 
     @pl.when(jnp.logical_not(has_up))
     def _():
-        v_buf[:, halo + tok_slab :, :] = jnp.zeros((chunks, halo, lanes), jnp.bfloat16)
+        kv_buf[1, :, halo + tok_slab :, :] = jnp.zeros((chunks, halo, lanes), jnp.bfloat16)
 
     lse_buf[...] = jnp.zeros(lse_buf.shape, jnp.float32)
-    for which, there in ((0, has_down), (1, has_up)):
-
-        def hear(which=which):
-            pl.semaphore_wait(beside.at[which], 1)
-            when(inner != across, lambda: tell_beside(which, {"head": inner}))
-
-        when(there, hear)
+    if slabs > 1:
+        heard = jnp.where(at_end, has_up.astype(jnp.int32) + has_down.astype(jnp.int32), 1)
+        pl.semaphore_wait(beside.at[0], heard)
+        when(inner != across, lambda: tell_beside({"head": inner}))
 
     mask_copy.wait()
     slot_copy.wait()
 
-    def wait_input(which, chunk):
-        _, buf, base = inputs[which]
-        wait_bytes(buf.at[chunk, pl.ds(base, tok_slab), :], in_recv.at[which, chunk])
-
     def forward(chunk):
         for which in range(2):
-            wait_input(which, chunk)
+            wait_bytes(kv_buf.at[which, chunk, pl.ds(halo, tok_slab), :], in_recv.at[which, chunk])
             when(has_up, lambda which=which: halo_copy(which, chunk, True).start())
             when(has_down, lambda which=which: halo_copy(which, chunk, False).start())
 
     def attend(chunk):
-        for which in range(2):
-            when(has_down, lambda which=which: halo_copy(which, chunk, True).wait_recv())
-            when(has_up, lambda which=which: halo_copy(which, chunk, False).wait_recv())
-        wait_input(2, chunk)
+        per_sides(lambda n: wait_bytes(kv_buf.at[:, chunk, pl.ds(0, n * halo), :], halo_recv.at[chunk]))
+        wait_bytes(q_buf.at[chunk], in_recv.at[2, chunk])
         for within in range(width):
             column = slice(within * head_dim, (within + 1) * head_dim)
             local_head = chunk * width + within
@@ -576,8 +570,8 @@
                 q_rows = slice(block * tile, (block + 1) * tile)
                 queries = q_buf[chunk, q_rows, column]
                 window = slice(block * tile, (block + band) * tile)
-                keys = k_buf[chunk, window, column]
-                values = v_buf[chunk, window, column]
+                keys = kv_buf[0, chunk, window, column]
+                values = kv_buf[1, chunk, window, column]
                 scores = (
                     lax.dot_general(
                         keys, queries, (((1,), (1,)), ((), ())), preferred_element_type=jnp.float32
@@ -672,16 +666,11 @@
     for block in range(tiles_dev):
         slot_lse_ref[:, block * tile : (block + 1) * tile] = slot_lse[block]
 
-    others = (owners - 1) * capacity * head_dim
-    for which in range(3):
-        wait_bytes(inputs[which][0].at[:, pl.ds(0, others)], in_send.at[which])
-    for which in range(2):
-        edge = inputs[which][1].at[:, pl.ds(0, halo), :]
-        when(has_up, lambda which=which, edge=edge: wait_bytes(edge, halo_send.at[which, 1]))
-        when(has_down, lambda which=which, edge=edge: wait_bytes(edge, halo_send.at[which, 0]))
-    wait_bytes(half, lse_send.at[owners])
+    wait_bytes(kv_buf.at[:, :, pl.ds(0, 3 * (owners - 1) * tok_dev // 2), :], in_send.at[0])
+    per_sides(lambda n: wait_bytes(kv_buf.at[:, :, pl.ds(0, n * halo), :], halo_send.at[0]))
+    wait_bytes(half, lse_send.at[0])
     when(inner == across, lambda: per_mate(lambda other: lse_relay(other).wait_send()))
-    wait_bytes(last_box.at[pl.ds(0, owners - 1)], lse_send.at[owners + 1])
+    wait_bytes(last_box.at[pl.ds(0, owners - 1)], lse_send.at[2])
     wait_bytes(o_buf.at[:, pl.ds(0, (owners - 1) * tok_dev), :], out_send.at[0])
     wait_bytes(out_ref, out_recv.at[0])
 
@@ -711,16 +700,10 @@
     whole = heads == owners * capacity
     width = HEADS_PER_CHUNK if whole and capacity % HEADS_PER_CHUNK == 0 else 1
     chunks = capacity // width
-    line = whole and owners % 2 == 0 and chunks > 1
+    line = whole and owners % 2 == 0 and owners <= 4 and chunks > 1 and 4 * halo >= tok_slab
     lanes = width * head_dim
     dims = (heads, head_dim, capacity, width, tok_dev, tile, reach)
     dma = pltpu.SemaphoreType.DMA
-    buffers = [
-        pltpu.VMEM((chunks, tok_slab, lanes), jnp.bfloat16),
-        pltpu.VMEM((chunks, tok_slab + 2 * halo, lanes), jnp.bfloat16),
-        pltpu.VMEM((chunks, tok_slab + 2 * halo, lanes), jnp.bfloat16),
-        pltpu.VMEM((chunks, tok_slab, lanes), jnp.bfloat16),
-    ]
     tables = [
         pltpu.SMEM((band, tiles_dev, heads), jnp.int32),
         pltpu.SMEM((heads,), jnp.int32),
@@ -730,27 +713,32 @@
         first_rows = (capacity - width) * tiles_dev
         last_rows = -(-width * tiles_dev // 8) * 8
         scratch = [
-            *buffers,
+            pltpu.VMEM((chunks, tok_slab, lanes), jnp.bfloat16),
+            pltpu.VMEM((2, chunks, tok_slab + 2 * halo, lanes), jnp.bfloat16),
+            pltpu.VMEM((chunks, tok_slab, lanes), jnp.bfloat16),
             pltpu.VMEM((first_rows + last_rows, tile), jnp.float32),
             pltpu.VMEM((owners, first_rows, tile), jnp.bfloat16),
             pltpu.VMEM((owners, last_rows, tile), jnp.bfloat16),
             *tables,
-            dma((3,)),
+            dma((1,)),
             dma((3, chunks)),
-            dma((2, 2)),
-            dma((2, chunks, 2)),
+            dma((1,)),
+            dma((chunks,)),
             dma((1,)),
             dma((1,)),
-            dma((owners + 2,)),
+            dma((3,)),
             dma((3,)),
             pltpu.SemaphoreType.REGULAR((owners,)),
-            pltpu.SemaphoreType.REGULAR((2,)),
+            pltpu.SemaphoreType.REGULAR((1,)),
             dma((2,)),
         ]
     else:
         kernel = attention_kernel
         scratch = [
-            *buffers,
+            pltpu.VMEM((chunks, tok_slab, lanes), jnp.bfloat16),
+            pltpu.VMEM((chunks, tok_slab + 2 * halo, lanes), jnp.bfloat16),
+            pltpu.VMEM((chunks, tok_slab + 2 * halo, lanes), jnp.bfloat16),
+            pltpu.VMEM((chunks, tok_slab, lanes), jnp.bfloat16),
             pltpu.VMEM((owners, capacity, 1, tok_slab), jnp.float32),
             *tables,
             dma((3, chunks, owners)),

time: 61.6 us -> 61.5 us (level)
  no operation moved by 1% of the time
where the time goes in v5:
time: 61.5 us; the launch traced here: 61.3 us
  Pallas kernels  60.7 us (99%)
  between operations  0.64 us (1%)
    pallas_call x1, Pallas kernels, on_device(): pl.pallas_call(functools.partial(kernel, owners, slabs, dims), out_shape=...  59.8 us

profile of v5, /device:TPU:9, one launch (start us, length us, event | category | flops | bytes accessed | tf_op | source)
XLA Modules:
  0.0 61.3 jit_solution(2434374838274995051)
XLA Ops:
  0.6 59.8 %shard_map.68 = (bf16[64,5120]{1,0:T(8,128)(2,1)S(1)}, f32[10,256]{1,0:T(8,128)S(1)}) custom-call(bf16[64,5120]{1,0:T(8,128)(2,1)} %q_ref.1, bf16[64,5120]{1,0:T(8,128)(2,1)} %k_ref.1, bf16[64,5120]{1,0:T(8,128)(2,1)} %v_ref.1, s32[5,2,40]{2,1,0:T(2,128)} %bitcast.1, s32[40]{0:T(128)} %slot_ref.1), custom_call_target="tpu_custom_call" | custom-call | tf_op jit(solution)/shard_map/pallas_call | solution.py:754
  60.5 0.9 %shard_map.69 = (bf16[64,5120]{1,0:T(8,128)(2,1)}, f32[10,256]{1,0:T(8,128)}) custom-call(bf16[64,5120]{1,0:T(8,128)(2,1)S(1)} %get-tuple-element.4.out_in, f32[10,256]{1,0:T(8,128)S(1)} %get-tuple-element.5.lse_in), custom_call_target="tpu_custom_call" | custom-call | tf_op jit(solution)/shard_map/pallas_call | solution.py:767

commit v6 on v5

--- a/solution.py
+++ b/solution.py
@@ -9,7 +9,7 @@
 
 MESH = pl.DeviceIdType.MESH
 HEADS_PER_CHUNK = 2
-EARLY_CHUNKS = 3
+EARLY_CHUNKS = 4
 QUERY_LAG = 0
 HELD_CHUNKS = 3
 FLOOR = -1e30
@@ -477,13 +477,14 @@
 
     mask_copy = pltpu.make_async_copy(mask_ref, mask_buf, small_sem.at[0])
     slot_copy = pltpu.make_async_copy(slot_ref, slot_buf, small_sem.at[1])
-    mask_copy.start()
-    slot_copy.start()
     pl.semaphore_wait(barrier, 1 + end_up.astype(jnp.int32) + end_down.astype(jnp.int32))
 
     for chunk in range(early):
         for which in range(3):
             in_copy(which, chunk, inner).start()
+
+    mask_copy.start()
+    slot_copy.start()
 
     def tell(owner, about):
         pl.semaphore_signal(seen.at[about], inc=1, device_id={"head": owner}, device_id_type=MESH)

time: 61.5 us -> 61.3 us (level)
  no operation moved by 1% of the time
where the time goes in v6:
time: 61.3 us; the launch traced here: 61.2 us
  Pallas kernels  60.5 us (99%)
  between operations  0.64 us (1%)
    pallas_call x1, Pallas kernels, on_device(): pl.pallas_call(functools.partial(kernel, owners, slabs, dims), out_shape=...  59.7 us

profile of v6, /device:TPU:9, one launch (start us, length us, event | category | flops | bytes accessed | tf_op | source)
XLA Modules:
  0.0 61.2 jit_solution(130739112001043067)
XLA Ops:
  0.6 59.7 %shard_map.68 = (bf16[64,5120]{1,0:T(8,128)(2,1)S(1)}, f32[10,256]{1,0:T(8,128)S(1)}) custom-call(bf16[64,5120]{1,0:T(8,128)(2,1)} %q_ref.1, bf16[64,5120]{1,0:T(8,128)(2,1)} %k_ref.1, bf16[64,5120]{1,0:T(8,128)(2,1)} %v_ref.1, s32[5,2,40]{2,1,0:T(2,128)} %bitcast.1, s32[40]{0:T(128)} %slot_ref.1), custom_call_target="tpu_custom_call" | custom-call | tf_op jit(solution)/shard_map/pallas_call | solution.py:755
  60.3 0.9 %shard_map.69 = (bf16[64,5120]{1,0:T(8,128)(2,1)}, f32[10,256]{1,0:T(8,128)}) custom-call(bf16[64,5120]{1,0:T(8,128)(2,1)S(1)} %get-tuple-element.4.out_in, f32[10,256]{1,0:T(8,128)S(1)} %get-tuple-element.5.lse_in), custom_call_target="tpu_custom_call" | custom-call | tf_op jit(solution)/shard_map/pallas_call | solution.py:768

commit v7 on v6

--- a/solution.py
+++ b/solution.py
@@ -9,7 +9,7 @@
 
 MESH = pl.DeviceIdType.MESH
 HEADS_PER_CHUNK = 2
-EARLY_CHUNKS = 4
+EARLY_CHUNKS = 3
 QUERY_LAG = 0
 HELD_CHUNKS = 3
 FLOOR = -1e30
@@ -324,6 +324,7 @@
     lse_buf,
     lse_box,
     last_box,
+    first_buf,
     mask_buf,
     slot_buf,
     in_send,
@@ -336,6 +337,7 @@
     lse_recv,
     seen,
     beside,
+    first_sem,
     small_sem,
 ):
     heads, head_dim, capacity, width, tok_dev, tile, reach = dims
@@ -378,10 +380,10 @@
     def wait_bytes(ref, sem):
         pltpu.make_async_copy(ref, ref, sem).wait()
 
-    def in_copy(which, chunk, dst_owner):
+    def in_copy(which, chunk, dst_owner, source=None):
         ref, buf, base = inputs[which]
         return pltpu.make_async_remote_copy(
-            src_ref=ref.at[:, columns(dst_owner, chunk)],
+            src_ref=ref.at[:, columns(dst_owner, chunk)] if source is None else source,
             dst_ref=buf.at[chunk, rows(me, base), :],
             send_sem=in_send.at[0],
             recv_sem=in_recv.at[which, chunk],
@@ -477,9 +479,27 @@
 
     mask_copy = pltpu.make_async_copy(mask_ref, mask_buf, small_sem.at[0])
     slot_copy = pltpu.make_async_copy(slot_ref, slot_buf, small_sem.at[1])
+    def stage():
+        for which in range(3):
+            pltpu.make_async_copy(
+                inputs[which][0].at[:, columns(inner, 0)], first_buf.at[which], first_sem.at[0]
+            ).start()
+
+    when(low, stage)
     pl.semaphore_wait(barrier, 1 + end_up.astype(jnp.int32) + end_down.astype(jnp.int32))
 
-    for chunk in range(early):
+    def begin_staged():
+        wait_bytes(first_buf, first_sem.at[0])
+        for which in range(3):
+            in_copy(which, 0, inner, first_buf.at[which]).start()
+
+    def begin():
+        for which in range(3):
+            in_copy(which, 0, inner).start()
+
+    when(low, begin_staged)
+    when(jnp.logical_not(low), begin)
+    for chunk in range(1, early):
         for which in range(3):
             in_copy(which, chunk, inner).start()
 
@@ -720,6 +740,7 @@
             pltpu.VMEM((first_rows + last_rows, tile), jnp.float32),
             pltpu.VMEM((owners, first_rows, tile), jnp.bfloat16),
             pltpu.VMEM((owners, last_rows, tile), jnp.bfloat16),
+            pltpu.VMEM((3, tok_dev, lanes), jnp.bfloat16),
             *tables,
             dma((1,)),
             dma((3, chunks)),
@@ -731,6 +752,7 @@
             dma((3,)),
             pltpu.SemaphoreType.REGULAR((owners,)),
             pltpu.SemaphoreType.REGULAR((1,)),
+            dma((1,)),
             dma((2,)),
         ]
     else:

time: 61.3 us -> 61.3 us (level)
  no operation moved by 1% of the time
where the time goes in v7:
time: 61.3 us; the launch traced here: 61.1 us
  Pallas kernels  60.5 us (99%)
  between operations  0.64 us (1%)
    pallas_call x1, Pallas kernels, on_device(): pl.pallas_call(functools.partial(kernel, owners, slabs, dims), out_shape=...  59.6 us

profile of v7, /device:TPU:9, one launch (start us, length us, event | category | flops | bytes accessed | tf_op | source)
XLA Modules:
  0.0 61.1 jit_solution(488054731234454141)
XLA Ops:
  0.6 59.6 %shard_map.68 = (bf16[64,5120]{1,0:T(8,128)(2,1)S(1)}, f32[10,256]{1,0:T(8,128)S(1)}) custom-call(bf16[64,5120]{1,0:T(8,128)(2,1)} %q_ref.1, bf16[64,5120]{1,0:T(8,128)(2,1)} %k_ref.1, bf16[64,5120]{1,0:T(8,128)(2,1)} %v_ref.1, s32[5,2,40]{2,1,0:T(2,128)} %bitcast.1, s32[40]{0:T(128)} %slot_ref.1), custom_call_target="tpu_custom_call" | custom-call | tf_op jit(solution)/shard_map/pallas_call | solution.py:777
  60.3 0.9 %shard_map.69 = (bf16[64,5120]{1,0:T(8,128)(2,1)}, f32[10,256]{1,0:T(8,128)}) custom-call(bf16[64,5120]{1,0:T(8,128)(2,1)S(1)} %get-tuple-element.4.out_in, f32[10,256]{1,0:T(8,128)S(1)} %get-tuple-element.5.lse_in), custom_call_target="tpu_custom_call" | custom-call | tf_op jit(solution)/shard_map/pallas_call | solution.py:790

commit v8 on v7

--- a/solution.py
+++ b/solution.py
@@ -246,7 +246,7 @@
                     (((0,), (0,)), ((), ())),
                     preferred_element_type=jnp.float32,
                 )
-                result = jnp.transpose(summed / total)
+                result = jnp.transpose(summed * (1.0 / total))
                 o_buf[chunk, q_rows, column] = result.astype(jnp.bfloat16)
                 lse_buf[me, local_head, :, q_rows] = highest + jnp.log(total)
 
@@ -618,7 +618,7 @@
                     (((0,), (0,)), ((), ())),
                     preferred_element_type=jnp.float32,
                 )
-                result = jnp.transpose(summed / total)
+                result = jnp.transpose(summed * (1.0 / total))
                 o_buf[chunk, q_rows, column] = result.astype(jnp.bfloat16)
                 row = local_head * tiles_dev + block
                 lse_buf[pl.ds(row, 1), :] = highest + jnp.log(total)

time: 61.3 us -> 61.3 us (level)
  no operation moved by 1% of the time
where the time goes in v8:
time: 61.3 us; the launch traced here: 61.1 us
  Pallas kernels  60.5 us (99%)
  between operations  0.64 us (1%)
    pallas_call x1, Pallas kernels, on_device(): pl.pallas_call(functools.partial(kernel, owners, slabs, dims), out_shape=...  59.6 us

profile of v8, /device:TPU:9, one launch (start us, length us, event | category | flops | bytes accessed | tf_op | source)
XLA Modules:
  0.0 61.1 jit_solution(488054731234454141)
XLA Ops:
  0.6 59.6 %shard_map.68 = (bf16[64,5120]{1,0:T(8,128)(2,1)S(1)}, f32[10,256]{1,0:T(8,128)S(1)}) custom-call(bf16[64,5120]{1,0:T(8,128)(2,1)} %q_ref.1, bf16[64,5120]{1,0:T(8,128)(2,1)} %k_ref.1, bf16[64,5120]{1,0:T(8,128)(2,1)} %v_ref.1, s32[5,2,40]{2,1,0:T(2,128)} %bitcast.1, s32[40]{0:T(128)} %slot_ref.1), custom_call_target="tpu_custom_call" | custom-call | tf_op jit(solution)/shard_map/pallas_call | solution.py:777
  60.3 0.9 %shard_map.69 = (bf16[64,5120]{1,0:T(8,128)(2,1)}, f32[10,256]{1,0:T(8,128)}) custom-call(bf16[64,5120]{1,0:T(8,128)(2,1)S(1)} %get-tuple-element.4.out_in, f32[10,256]{1,0:T(8,128)S(1)} %get-tuple-element.5.lse_in), custom_call_target="tpu_custom_call" | custom-call | tf_op jit(solution)/shard_map/pallas_call | solution.py:790
